TPU v7x, 256 devices: a whole 4x4x8 slice. The times are simulated.
256 devices in a mesh: coh: 4 (over y), lat: 4 (over x), lon: 16 (over z, core).
Axes of the slice: x: 4, y: 4, z: 8, core: 2. Of those that a mesh axis runs over, the one named last changes fastest.
Arguments:
- saved_period_abundance: bfloat16 [2, 128, 256, 4096], P(None, 'coh', 'lat', 'lon'), may hold values from 0.099609375 to 2
- final_abundance_sensitivity: bfloat16 [128, 256, 4096], P('coh', 'lat', 'lon'), may hold values from -6 to 6
- prey_biomass: float32 [2, 256, 4096], P(None, 'lat', 'lon'), may hold values from 0.2 to 2
- water_heat_field: float32 [2, 256, 4096], P(None, 'lat', 'lon'), may hold values from 10 to 30
- marine_indicator: int32 [256, 4096], P('lat', 'lon'), may hold values 0 or 1
- fishing_pressure: float32 [256, 4096], P('lat', 'lon'), may hold values from 0.1 to 2
- offspring_yield: float32 [256, 4096], P('lat', 'lon'), may hold values from 2 to 20
- death_fraction: float32 [128], P('coh'), may hold values from 0.01 to 0.5
- gear_vulnerability: float32 [128], P('coh'), may hold values from 0.05 to 0.5
- spreading_coefficient: float32 [128], P('coh'), may hold values from 0.02 to 0.12
- directed_drift_rate: float32 [128], P('coh'), may hold values from 0.01 to 0.06
- favoured_thermal_level: float32 [128], P('coh'), may hold values from 12 to 28
- breeding_contribution: float32 [128], P('coh'), may hold values from 0.005 to 0.03
- landing_error_sensitivity: float32 [2048, 2, 128], P(('lat', 'lon'), None, 'coh'), may hold values from -6 to 6
- fleet_east_piece: int32 [2048, 1], P(('lat', 'lon')), may hold values from 0 to 15; in each aligned block of 32 rows (0 to 31, 32 to 63, ...) at most 3 rows name the same one
- fleet_north_piece: int32 [2048], P(('lat', 'lon')), may hold values from 0 to 3
- fleet_area_patch: int32 [2048], P(('lat', 'lon')), may hold values from 0 to 31
- fleet_age_bounds: int32 [2048, 2], P(('lat', 'lon')), may hold values from 0 to 128, as said below
Outputs:
- density_grad: float32 [128, 256, 4096], P('coh', 'lat', 'lon')
- recruit_grad: float32 [256, 4096], P('lat', 'lon')
Inputs may be any that keep to these rules, and one draw needn't show every extreme that they name: `fleet_east_piece`: among the rows of one device, at most 3 name the same longitude tile, and some longitude tile is named by exactly 3 of them. `fleet_age_bounds`: in every row the first entry is below the second.
All inputs are finite; a program needn't handle non-finite values. No bound on the sum of `marine_indicator` on one device may be relied on, other than what follows from the above.
Results may differ from a plain program's by a relative error of at most 0.0003.
Values sent between devices are 32-bit elements; how exact they have to be, the bound alone decides.
A program may use at most 64 MiB of HBM per device.

v0:
```python
import jax
import jax.numpy as jnp
from jax import lax
from jax.sharding import PartitionSpec as P

BY = 16
BX = 32
thermal_tolerance_spread = 4.0
highest = lax.Precision.HIGHEST


def from_root(value, axis, source):
    kept = jnp.where(lax.axis_index(axis) == source, value, 0).astype(value.dtype)
    return lax.psum(kept, axis)


def shifted(block, axis, distance):
    devices = range(lax.axis_size(axis))
    route = [(i - distance, i) for i in devices if i - distance in devices]
    return lax.ppermute(block, axis, route)


def with_halo(x, sides, width):
    for axis, dim in sides:
        devices, length = (lax.axis_size(axis), x.shape[dim])
        up = [(i, (i + 1) % devices) for i in range(devices - 1)]
        down = [(j, i) for i, j in up]
        last = lax.slice_in_dim(x, length - width, length, axis=dim)
        first = lax.slice_in_dim(x, 0, width, axis=dim)
        before = lax.ppermute(last, axis, up)
        after = lax.ppermute(first, axis, down)
        x = jnp.concatenate([before, x, after], axis=dim)
    return x


def views(rimmed):
    return (
        rimmed[..., :-2, 1:-1],
        rimmed[..., 2:, 1:-1],
        rimmed[..., 1:-1, 2:],
        rimmed[..., 1:-1, :-2],
    )


def fold_rows(base, nblocks, pieces):
    values, targets = pieces
    wanted = (base + jnp.arange(nblocks)).astype(jnp.float32)
    onehot = (targets[None, :] == wanted[:, None]).astype(jnp.float32)
    return jnp.dot(onehot, values, precision=highest)


def shards(
    saved_period_abundance,
    final_abundance_sensitivity,
    prey_biomass,
    water_heat_field,
    marine_indicator,
    fishing_pressure,
    offspring_yield,
    death_fraction,
    gear_vulnerability,
    spreading_coefficient,
    directed_drift_rate,
    favoured_thermal_level,
    breeding_contribution,
    landing_error_sensitivity,
    fleet_east_piece,
    fleet_north_piece,
    fleet_area_patch,
    fleet_age_bounds,
):
    months, ages_here, rows_y, rows_x = saved_period_abundance.shape
    coh_pos = lax.axis_index("coh")
    lat_pos = lax.axis_index("lat")
    lon_pos = lax.axis_index("lon")
    lon_count = lax.axis_size("lon")
    total_ages = ages_here * lax.axis_size("coh")
    cohort_age = coh_pos * ages_here + jnp.arange(ages_here)
    maturity = (cohort_age + 1).astype(jnp.float32) / total_ages * breeding_contribution
    sea_field = marine_indicator.astype(jnp.float32)
    row_count = landing_error_sensitivity.shape[0]
    blocks_y = rows_y // BY
    blocks_x = rows_x // BX
    nblocks = blocks_y * blocks_x
    inside = (cohort_age[None, :] >= fleet_age_bounds[:, 0:1]) & (
        cohort_age[None, :] < fleet_age_bounds[:, 1:2]
    )
    masked = (landing_error_sensitivity * inside[:, None, :].astype(jnp.float32)).reshape(
        row_count, months * ages_here
    )
    place_id = (
        (fleet_north_piece * lon_count + fleet_east_piece[:, 0]) * nblocks + fleet_area_patch
    ).astype(jnp.float32)
    block_values = fold_rows(
        (lat_pos * lon_count + lon_pos) * nblocks,
        nblocks,
        (
            lax.all_gather(masked, ("lat", "lon"), axis=0, tiled=True),
            lax.all_gather(place_id, ("lat", "lon"), axis=0, tiled=True),
        ),
    )
    partial_spawn = jnp.stack(
        [
            jnp.tensordot(
                maturity,
                saved_period_abundance[period_counter].astype(jnp.float32),
                axes=1,
                precision=highest,
            )
            for period_counter in range(months)
        ]
    )
    survive = jnp.exp(
        -death_fraction[:, None, None] - gear_vulnerability[:, None, None] * fishing_pressure[None]
    )
    adjoint = final_abundance_sensitivity.astype(jnp.float32)
    grad_recruit = jnp.zeros((rows_y, rows_x), jnp.float32)
    spawn_total = lax.psum(partial_spawn, "coh")
    for period_counter in range(months - 1, -1, -1):
        spawning = spawn_total[period_counter]
        first_plane = from_root(adjoint[0], "coh", 0)
        next_plane = shifted(adjoint[0], "coh", -1)
        extended = jnp.concatenate(
            [
                adjoint[1:],
                next_plane[None],
                prey_biomass[period_counter][None],
                water_heat_field[period_counter][None],
                sea_field[None],
            ],
            axis=0,
        )
        rimmed = with_halo(extended, (("lat", 1), ("lon", 2)), 1)
        later_rim = rimmed[:ages_here]
        forage_rim = rimmed[ages_here]
        thermal_halo_border = rimmed[ages_here + 1]
        sea_rim = rimmed[ages_here + 2]
        thermal_departure = (
            thermal_halo_border[None] - favoured_thermal_level[:, None, None]
        ) / thermal_tolerance_spread
        habitat = sea_rim * forage_rim / (1.0 + thermal_departure * thermal_departure)
        later = later_rim[:, 1:-1, 1:-1]
        habitat_here = habitat[:, 1:-1, 1:-1]
        outflow = jnp.zeros_like(later)
        for sea_next, hab_next, adj_next in zip(views(sea_rim), views(habitat), views(later_rim)):
            flow_rate = (
                sea_field
                * sea_next
                * (
                    spreading_coefficient[:, None, None]
                    + jnp.maximum(
                        directed_drift_rate[:, None, None] * (hab_next - habitat_here), 0.0
                    )
                )
            )
            outflow = outflow + flow_rate * (later - adj_next)
        after_move = later - outflow
        ratio = 1.0 / (1.0 + spawning)
        recruit_term = first_plane * sea_field * offspring_yield * ratio * ratio
        month_values = block_values[
            :, period_counter * ages_here : (period_counter + 1) * ages_here
        ]
        block_grid = month_values.reshape(blocks_y, blocks_x, ages_here).transpose(2, 0, 1)
        spread = jnp.broadcast_to(
            block_grid[:, :, None, :, None], (ages_here, blocks_y, BY, blocks_x, BX)
        )
        adjoint = (
            survive * after_move
            + recruit_term[None] * maturity[:, None, None]
            + gear_vulnerability[:, None, None]
            * fishing_pressure[None]
            * spread.reshape(ages_here, rows_y, rows_x)
        )
        grad_recruit = grad_recruit + first_plane * sea_field * spawning * ratio
    return (adjoint, grad_recruit)


def solution(mesh):
    in_specs = (
        P(None, "coh", "lat", "lon"),
        P("coh", "lat", "lon"),
        P(None, "lat", "lon"),
        P(None, "lat", "lon"),
        P("lat", "lon"),
        P("lat", "lon"),
        P("lat", "lon"),
        P("coh"),
        P("coh"),
        P("coh"),
        P("coh"),
        P("coh"),
        P("coh"),
        P(("lat", "lon"), None, "coh"),
        P(("lat", "lon"), None),
        P(("lat", "lon")),
        P(("lat", "lon")),
        P(("lat", "lon"), None),
    )
    out_specs = (P("coh", "lat", "lon"), P("lat", "lon"))
    return jax.shard_map(shards, mesh=mesh, in_specs=in_specs, out_specs=out_specs, check_vma=False)
```

profile of v0, /device:TPU:2, one launch (start us, length us, event | category | flops | bytes accessed | tf_op | source)
XLA Modules:
  0.0 357.3 jit_solution(8194302968326700372)
XLA Ops:
  15.1 1.8 constant_dynamic-update-slice_fusion.1
  17.1 53.0 %all_gather.7 = f32[2048,64]{1,0:T(8,128)S(1)} all-gather(f32[32,64]{1,0:T(8,128)S(1)} %reshape.100), channel_id=1, replica_groups=mesh['coh'=4,'lat'=4,'lon'=16] {'lat','lon'}, dimensions={0}, use_global_device_ids=true | all-gather | bytes 532480 | tf_op jit(solution)/shard_map/all_gather | solution.py:98
  72.9 109.3 %all-reduce = f32[2048]{0:T(1024)S(1)} all-reduce(f32[2048]{0:T(1024)S(1)} %convert_dynamic-update-slice_fusion), channel_id=1, replica_groups=mesh['coh'=4,'lat'=4,'lon'=16] {'lat','lon'}, use_global_device_ids=true, to_apply=%add | all-reduce | flops 2048 | bytes 16384
  184.1 22.3 %collective-permute-start.2 = (f32[35,1,256]{2,1,0:T(1,128)S(1)}, f32[35,1,256]{2,1,0:T(1,128)S(1)}, u32[]{:S(2)}, u32[]{:S(2)}) collective-permute-start(f32[35,1,256]{2,1,0:T(1,128)S(1)} %get-tuple-element.17), channel_id=1, source_target_pairs={{16,0},{32,16},{48,32},{17,1},{33,17},{49,33},{18,2},{34,18},{50,3... | collective-permute-start | bytes 107528 | tf_op jit(solution)/shard_map/ppermute | solution.py:31
  206.4 1.9 collective-permute-start.1
  208.8 3.4 collective-permute-done.1
  212.6 1.9 fusion.82
  214.5 1.9 copy.35
  217.6 1.8 copy.36
  222.7 3.9 %broadcast_in_dim.18 = f32[32,4,16,8,32]{4,3,2,1,0:T(8,128)} broadcast(f32[32,4,8]{2,1,0:T(4,128)S(1)} %copy.41), dimensions={0,1,3} | broadcast | bytes 2101248 | tf_op jit(solution)/shard_map/broadcast_in_dim | solution.py:164
  226.6 7.0 %reshape.102 = f32[32,64,256]{2,1,0:T(8,128)} reshape(f32[32,4,16,8,32]{4,3,2,1,0:T(8,128)} %broadcast_in_dim.18) | data formatting | bytes 4194304 | tf_op jit(solution)/shard_map/reshape | solution.py:172
  242.0 13.6 %fusion.4 = f32[32,64,256]{2,1,0:T(8,128)S(1)} fusion(f32[32,64,256]{2,1,0:T(8,128)} %reshape.102, f32[35,66,1]{2,1,0:T(8,128)} %copy.37, f32[35,1,256]{2,1,0:T(1,128)} %copy-done.12, f32[35,64,256]{2,1,0:T(8,128)} %copy-done, f32[35,1,256]{2,1,0:T(1,128)} %copy-done.14, f32[32,66,258]{2,1,0:T(8,128)S(1)} %add_divide_fusion.1, f32[35,66,1]{2,1,0:T(8,128)} %copy.38, ...), kind=kLoop, calls=%fused_computation.11 | loop fusion | flops 25165824 | bytes 19554992 | tf_op jit(solution)/shard_map/add | solution.py:168
  257.0 1.8 fusion.85
  258.8 4.0 %collective-permute-done.5 = f32[64,256]{1,0:T(8,128)S(1)} collective-permute-done((f32[64,256]{1,0:T(8,128)S(1)}, f32[64,256]{1,0:T(8,128)S(1)}, u32[]{:S(2)}, u32[]{:S(2)}) %collective-permute-start.5) | collective-permute-done | bytes 65568 | tf_op jit(solution)/shard_map/ppermute | solution.py:20
  262.9 1.9 collective-permute-start.7
  264.8 3.9 %collective-permute-start.6 = (f32[35,1,256]{2,1,0:T(1,128)S(1)}, f32[35,1,256]{2,1,0:T(1,128)S(1)}, u32[]{:S(2)}, u32[]{:S(2)}) collective-permute-start(f32[35,1,256]{2,1,0:T(1,128)S(1)} %get-tuple-element.14), channel_id=1, source_target_pairs={{0,16},{16,32},{32,48},{1,17},{17,33},{33,49},{2,18},{18,34},{34,5... | collective-permute-start | bytes 107528 | tf_op jit(solution)/shard_map/ppermute | solution.py:30
  268.9 3.9 %broadcast_in_dim.20 = f32[32,4,16,8,32]{4,3,2,1,0:T(8,128)} broadcast(f32[32,4,8]{2,1,0:T(4,128)S(1)} %copy.48), dimensions={0,1,3} | broadcast | bytes 2101248 | tf_op jit(solution)/shard_map/broadcast_in_dim | solution.py:164
  272.8 7.0 %reshape.104 = f32[32,64,256]{2,1,0:T(8,128)} reshape(f32[32,4,16,8,32]{4,3,2,1,0:T(8,128)} %broadcast_in_dim.20) | data formatting | bytes 4194304 | tf_op jit(solution)/shard_map/reshape | solution.py:172
  280.2 1.9 fusion.81
  282.1 1.8 copy.42
  285.4 1.8 copy.43
  296.8 37.3 %all-reduce.5.cloned.1.call-done = f32[64,256]{1,0:T(8,128)} async-done(((f32[64,256]{1,0:T(8,128)}), f32[64,256]{1,0:T(8,128)}) %all-reduce.5.cloned.1.call-update) | async-done | bytes 65552 | tf_op jit(solution)/shard_map/psum | solution.py:14
  334.1 1.9 multiply_add_fusion
  336.1 14.3 %fusion.6 = f32[32,64,256]{2,1,0:T(8,128)} fusion(f32[32,64,256]{2,1,0:T(8,128)} %reshape.104, f32[35,66,1]{2,1,0:T(8,128)} %copy.44, f32[35,1,256]{2,1,0:T(1,128)} %copy-done.11, f32[35,64,256]{2,1,0:T(8,128)} %copy-done.1, f32[35,1,256]{2,1,0:T(1,128)} %copy-done.13, f32[32,66,258]{2,1,0:T(8,128)S(1)} %add_divide_fusion, f32[35,66,1]{2,1,0:T(8,128)} %copy.45, ...), kind=kLoop, calls=%fused_computation.13 | loop fusion | flops 25165824 | bytes 19554992 | tf_op jit(solution)/shard_map/add | solution.py:168
  (129 shorter events, 38.6 us)
Async XLA Ops:
  7.2 233.5 %all-reduce.7.cloned.1.call-start = ((), (), s32[]{:S(2)}) async-start(), calls=%async_computation.1 | async-start | bytes 393216 | tf_op jit(solution)/shard_map/psum | solution.py:14
  8.7 173.6 %collective-permute-start = (f32[64,256]{1,0:T(8,128)S(1)}, f32[64,256]{1,0:T(8,128)S(1)}, u32[]{:S(2)}, u32[]{:S(2)}) collective-permute-start(f32[64,256]{1,0:T(8,128)S(1)} %slice_bitcast_fusion.5), channel_id=1, source_target_pairs={{64,0},{128,64},{192,128},{65,1},{129,65},{193,129},{66,2},{130,66... | collective-permute-start | bytes 196616 | tf_op jit(solution)/shard_map/ppermute | solution.py:20
  15.0 319.1 %all-reduce.5.cloned.1.call-start = ((), (), s32[]{:S(2)}) async-start(), calls=%async_computation | async-start | bytes 131072 | tf_op jit(solution)/shard_map/psum | solution.py:14
  15.1 168.9 %copy-start.9 = (s32[64,256]{1,0:T(8,128)S(1)}, s32[64,256]{1,0:T(8,128)}, u32[]{:S(2)}) copy-start(s32[64,256]{1,0:T(8,128)} %param.22) | copy-start | bytes 196612
  182.3 24.1 %copy-start.15 = (f32[64,256]{1,0:T(8,128)}, f32[64,256]{1,0:T(8,128)S(1)}, u32[]{:S(2)}) copy-start(f32[64,256]{1,0:T(8,128)S(1)} %collective-permute-done) | copy-start | bytes 196612
  184.0 54.4 %copy-start = (f32[35,64,256]{2,1,0:T(8,128)}, f32[35,64,256]{2,1,0:T(8,128)S(1)}, u32[]{:S(2)}) copy-start(f32[35,64,256]{2,1,0:T(8,128)S(1)} %bitcast_dynamic-update-slice_fusion.1) | copy-start | bytes 6881284
  184.1 24.7 %collective-permute-start.2 = (f32[35,1,256]{2,1,0:T(1,128)S(1)}, f32[35,1,256]{2,1,0:T(1,128)S(1)}, u32[]{:S(2)}, u32[]{:S(2)}) collective-permute-start(f32[35,1,256]{2,1,0:T(1,128)S(1)} %get-tuple-element.17), channel_id=1, source_target_pairs={{16,0},{32,16},{48,32},{17,1},{33,17},{49,33},{18,2},{34,18},{50,3... | collective-permute-start | bytes 107528 | tf_op jit(solution)/shard_map/ppermute | solution.py:31
  206.4 5.8 %collective-permute-start.1 = (f32[35,1,256]{2,1,0:T(1,128)S(1)}, f32[35,1,256]{2,1,0:T(1,128)S(1)}, u32[]{:S(2)}, u32[]{:S(2)}) collective-permute-start(f32[35,1,256]{2,1,0:T(1,128)S(1)} %get-tuple-element.16), channel_id=1, source_target_pairs={{0,16},{16,32},{32,48},{1,17},{17,33},{33,49},{2,18},{18,34},{34,5... | collective-permute-start | bytes 107528 | tf_op jit(solution)/shard_map/ppermute | solution.py:30
  208.8 29.6 %copy-start.12 = (f32[35,1,256]{2,1,0:T(1,128)}, f32[35,1,256]{2,1,0:T(1,128)S(1)}, u32[]{:S(2)}) copy-start(f32[35,1,256]{2,1,0:T(1,128)S(1)} %collective-permute-done.2) | copy-start | bytes 107524
  212.2 26.2 %copy-start.14 = (f32[35,1,256]{2,1,0:T(1,128)}, f32[35,1,256]{2,1,0:T(1,128)S(1)}, u32[]{:S(2)}) copy-start(f32[35,1,256]{2,1,0:T(1,128)S(1)} %collective-permute-done.1) | copy-start | bytes 107524
  216.3 17.9 %collective-permute-start.3 = (f32[35,66,1]{1,2,0:T(1,128)S(1)}, f32[35,66,1]{1,2,0:T(1,128)S(1)}, u32[]{:S(2)}, u32[]{:S(2)}) collective-permute-start(f32[35,66,1]{1,2,0:T(1,128)S(1)} %copy.35), channel_id=1, source_target_pairs={{0,1},{1,2},{2,3},{3,4},{4,5},{5,6},{6,7},{7,8},{8,9},{9,10},{10,1... | collective-permute-start | bytes 27728 | tf_op jit(solution)/shard_map/ppermute | solution.py:30
  219.4 16.4 %collective-permute-start.4 = (f32[35,66,1]{1,2,0:T(1,128)S(1)}, f32[35,66,1]{1,2,0:T(1,128)S(1)}, u32[]{:S(2)}, u32[]{:S(2)}) collective-permute-start(f32[35,66,1]{1,2,0:T(1,128)S(1)} %copy.36), channel_id=1, source_target_pairs={{1,0},{2,1},{3,2},{4,3},{5,4},{6,5},{7,6},{8,7},{9,8},{10,9},{11,1... | collective-permute-start | bytes 27728 | tf_op jit(solution)/shard_map/ppermute | solution.py:31
  255.6 7.2 %collective-permute-start.5 = (f32[64,256]{1,0:T(8,128)S(1)}, f32[64,256]{1,0:T(8,128)S(1)}, u32[]{:S(2)}, u32[]{:S(2)}) collective-permute-start(f32[64,256]{1,0:T(8,128)S(1)} %slice_bitcast_fusion.3), channel_id=1, source_target_pairs={{64,0},{128,64},{192,128},{65,1},{129,65},{193,129},{66,2},{130,66... | collective-permute-start | bytes 196616 | tf_op jit(solution)/shard_map/ppermute | solution.py:20
  262.8 31.7 %copy-start.1 = (f32[35,64,256]{2,1,0:T(8,128)}, f32[35,64,256]{2,1,0:T(8,128)S(1)}, u32[]{:S(2)}) copy-start(f32[35,64,256]{2,1,0:T(8,128)S(1)} %bitcast_dynamic-update-slice_fusion) | copy-start | bytes 6881284
  262.9 16.9 %collective-permute-start.7 = (f32[35,1,256]{2,1,0:T(1,128)S(1)}, f32[35,1,256]{2,1,0:T(1,128)S(1)}, u32[]{:S(2)}, u32[]{:S(2)}) collective-permute-start(f32[35,1,256]{2,1,0:T(1,128)S(1)} %get-tuple-element.15), channel_id=1, source_target_pairs={{16,0},{32,16},{48,32},{17,1},{33,17},{49,33},{18,2},{34,18},{50,3... | collective-permute-start | bytes 107528 | tf_op jit(solution)/shard_map/ppermute | solution.py:31
  264.8 15.0 %collective-permute-start.6 = (f32[35,1,256]{2,1,0:T(1,128)S(1)}, f32[35,1,256]{2,1,0:T(1,128)S(1)}, u32[]{:S(2)}, u32[]{:S(2)}) collective-permute-start(f32[35,1,256]{2,1,0:T(1,128)S(1)} %get-tuple-element.14), channel_id=1, source_target_pairs={{0,16},{16,32},{32,48},{1,17},{17,33},{33,49},{2,18},{18,34},{34,5... | collective-permute-start | bytes 107528 | tf_op jit(solution)/shard_map/ppermute | solution.py:30
  279.8 14.7 %copy-start.11 = (f32[35,1,256]{2,1,0:T(1,128)}, f32[35,1,256]{2,1,0:T(1,128)S(1)}, u32[]{:S(2)}) copy-start(f32[35,1,256]{2,1,0:T(1,128)S(1)} %collective-permute-done.7) | copy-start | bytes 107524
  279.8 14.7 %copy-start.13 = (f32[35,1,256]{2,1,0:T(1,128)}, f32[35,1,256]{2,1,0:T(1,128)S(1)}, u32[]{:S(2)}) copy-start(f32[35,1,256]{2,1,0:T(1,128)S(1)} %collective-permute-done.6) | copy-start | bytes 107524
  283.8 6.4 %collective-permute-start.8 = (f32[35,66,1]{1,2,0:T(1,128)S(1)}, f32[35,66,1]{1,2,0:T(1,128)S(1)}, u32[]{:S(2)}, u32[]{:S(2)}) collective-permute-start(f32[35,66,1]{1,2,0:T(1,128)S(1)} %copy.42), channel_id=1, source_target_pairs={{0,1},{1,2},{2,3},{3,4},{4,5},{5,6},{6,7},{7,8},{8,9},{9,10},{10,1... | collective-permute-start | bytes 27728 | tf_op jit(solution)/shard_map/ppermute | solution.py:30
  287.2 4.6 %collective-permute-start.9 = (f32[35,66,1]{1,2,0:T(1,128)S(1)}, f32[35,66,1]{1,2,0:T(1,128)S(1)}, u32[]{:S(2)}, u32[]{:S(2)}) collective-permute-start(f32[35,66,1]{1,2,0:T(1,128)S(1)} %copy.43), channel_id=1, source_target_pairs={{1,0},{2,1},{3,2},{4,3},{5,4},{6,5},{7,6},{8,7},{9,8},{10,9},{11,1... | collective-permute-start | bytes 27728 | tf_op jit(solution)/shard_map/ppermute | solution.py:31
  296.0 40.0 %copy-start.21 = (f32[32]{0:T(128)S(1)}, f32[32]{0:T(128)}, u32[]{:S(2)}) copy-start(f32[32]{0:T(128)} %copy-done.20) | copy-start | bytes 388
  296.0 40.0 %copy-start.22 = (f32[32]{0:T(128)S(1)}, f32[32]{0:T(128)}, u32[]{:S(2)}) copy-start(f32[32]{0:T(128)} %param.28) | copy-start | bytes 388
  296.0 40.0 %copy-start.23 = (f32[32]{0:T(128)S(1)}, f32[32]{0:T(128)}, u32[]{:S(2)}) copy-start(f32[32]{0:T(128)} %param.27) | copy-start | bytes 388
  296.0 40.0 %copy-start.24 = (f32[32]{0:T(128)S(1)}, f32[32]{0:T(128)}, u32[]{:S(2)}) copy-start(f32[32]{0:T(128)} %param.26) | copy-start | bytes 388
  (18 other events, 66.1 us)
Sparse Core Ops, SparseCore 0:
  15.2 50.9 all-reduce.6
  290.4 43.6 all-reduce.4
where the time goes:
time: 358 us; the launch traced here: 357 us
  blocking collectives  162 us (45%)
  local copies, waits for them, and re-layouts  51 us (14%)
  waiting for transfers between devices  44.8 us (13%)
  other arithmetic  42.6 us (12%)
  starting transfers between devices  38.8 us (11%)
  between operations  15.3 us (4%)
    unnamed x1, blocking collectives  109 us
    all_gather x1, blocking collectives, shards(): lax.all_gather(masked, ('lat', 'lon'), axis=0, tiled=True)  53 us
    psum x2, waiting for transfers between devices, from_root(): return lax.psum(kept, axis)  37.3 us
    add x2, other arithmetic, shards(): survive * after_move + recruit_term[None] * maturity[:, None, None]  27.9 us
    ppermute x4, starting transfers between devices, with_halo(): after = lax.ppermute(first, axis, down)  27.2 us
    reshape x2, local copies, waits for them, and re-layouts, shards(): spread.reshape(ages_here, rows_y, rows_x)  14.1 us
    ppermute x4, starting transfers between devices, with_halo(): before = lax.ppermute(last, axis, up)  8.77 us
    broadcast_in_dim x2, local copies, waits for them, and re-layouts, shards(): jnp.broadcast_to(block_grid[:, :, None, :, None], (ages_here, blocks_y, B...  7.82 us
  transfers between devices with their start and end apart: 12, of which 3 were waited for; matrix products, arithmetic and copies ran while one was open for 16% of the time, Pallas kernels for 0%

commit v1 on v0

--- a/solution.py
+++ b/solution.py
@@ -11,7 +11,7 @@
 
 def from_root(value, axis, source):
     kept = jnp.where(lax.axis_index(axis) == source, value, 0).astype(value.dtype)
-    return lax.psum(kept, axis)
+    return jnp.sum(lax.all_gather(kept, axis), axis=0)
 
 
 def shifted(block, axis, distance):

time: 358 us -> 342 us (0.955)
  waiting for transfers between devices: 44.8 us -> 6.94 us
  blocking collectives: 162 us -> 190 us
  other arithmetic: 42.6 us -> 34.6 us
    psum x2 -> x1, waiting for transfers between devices: 37.3 us -> 0.02 us  [shards(): spawn_total = lax.psum(partial_spawn, 'coh')]
    all_gather x0 -> x2, blocking collectives: none -> 27.6 us  [from_root(): return jnp.sum(lax.all_gather(kept, axis), axis=0)]
    add x2, other arithmetic: 27.9 us -> 22.5 us  [shards(): survive * after_move + recruit_term[None] * maturity[:, None, None]]
    unnamed x69 -> x75, local copies, waits for them, and re-layouts: 6.18 us -> 7.35 us
  transfers between devices with their start and end apart: 12 -> 11, of which waited for: 3 -> 2; matrix products, arithmetic and copies ran while one was open for 16% -> 16% of each run, Pallas kernels for 0% -> 0%
where the time goes in v1:
time: 342 us; the launch traced here: 341 us
  blocking collectives  190 us (56%)
  local copies, waits for them, and re-layouts  53.5 us (16%)
  starting transfers between devices  38 us (11%)
  other arithmetic  34.6 us (10%)
  between operations  15.3 us (4%)
  waiting for transfers between devices  6.94 us (2%)
    unnamed x1, blocking collectives  109 us
    all_gather x1, blocking collectives, shards(): lax.all_gather(masked, ('lat', 'lon'), axis=0, tiled=True)  53 us
    all_gather x2, blocking collectives, from_root(): return jnp.sum(lax.all_gather(kept, axis), axis=0)  27.6 us
    ppermute x4, starting transfers between devices, with_halo(): after = lax.ppermute(first, axis, down)  26.8 us
    add x2, other arithmetic, shards(): survive * after_move + recruit_term[None] * maturity[:, None, None]  22.5 us
    reshape x2, local copies, waits for them, and re-layouts, shards(): spread.reshape(ages_here, rows_y, rows_x)  14.1 us
    ppermute x4, starting transfers between devices, with_halo(): before = lax.ppermute(last, axis, up)  8.46 us
    slice x4, local copies, waits for them, and re-layouts, with_halo(): first = lax.slice_in_dim(x, 0, width, axis=dim)  7.96 us
  transfers between devices with their start and end apart: 11, of which 2 were waited for; matrix products, arithmetic and copies ran while one was open for 16% of the time, Pallas kernels for 0%

profile of v1, /device:TPU:2, one launch (start us, length us, event | category | flops | bytes accessed | tf_op | source)
XLA Modules:
  0.0 340.8 jit_solution(8174303705523858963)
XLA Ops:
  17.1 53.0 %all_gather.16 = f32[2048,64]{1,0:T(8,128)S(1)} all-gather(f32[32,64]{1,0:T(8,128)S(1)} %reshape.100), channel_id=1, replica_groups=mesh['coh'=4,'lat'=4,'lon'=16] {'lat','lon'}, dimensions={0}, use_global_device_ids=true | all-gather | bytes 532480 | tf_op jit(solution)/shard_map/all_gather | solution.py:98
  72.9 109.3 %all-reduce = f32[2048]{0:T(1024)S(1)} all-reduce(f32[2048]{0:T(1024)S(1)} %convert_dynamic-update-slice_fusion), channel_id=1, replica_groups=mesh['coh'=4,'lat'=4,'lon'=16] {'lat','lon'}, use_global_device_ids=true, to_apply=%add | all-reduce | flops 2048 | bytes 16384
  184.6 22.3 %collective-permute-start.2 = (f32[35,1,256]{2,1,0:T(1,128)S(1)}, f32[35,1,256]{2,1,0:T(1,128)S(1)}, u32[]{:S(2)}, u32[]{:S(2)}) collective-permute-start(f32[35,1,256]{2,1,0:T(1,128)S(1)} %get-tuple-element.15), channel_id=1, source_target_pairs={{16,0},{32,16},{48,32},{17,1},{33,17},{49,33},{18,2},{34,18},{50,3... | collective-permute-start | bytes 107528 | tf_op jit(solution)/shard_map/ppermute | solution.py:31
  206.9 1.9 collective-permute-start.1
  208.9 3.8 %collective-permute-done.1 = f32[35,1,256]{2,1,0:T(1,128)S(1)} collective-permute-done((f32[35,1,256]{2,1,0:T(1,128)S(1)}, f32[35,1,256]{2,1,0:T(1,128)S(1)}, u32[]{:S(2)}, u32[]{:S(2)}) %collective-permute-start.1) | collective-permute-done | bytes 35872 | tf_op jit(solution)/shard_map/ppermute | solution.py:30
  213.0 1.9 fusion.82
  215.0 1.9 copy.37
  218.1 2.4 copy.38
  221.8 15.0 %all_gather.14 = f32[4,64,256]{2,1,0:T(8,128)} all-gather(f32[1,64,256]{2,1,0:T(8,128)S(1)} %get-tuple-element.22), channel_id=1, replica_groups=mesh['coh'=4,'lat'=4,'lon'=16] {'coh'}, dimensions={0}, use_global_device_ids=true | all-gather | bytes 327680 | tf_op jit(solution)/shard_map/all_gather | solution.py:14
  238.5 3.9 %broadcast_in_dim.18 = f32[32,4,16,8,32]{4,3,2,1,0:T(8,128)} broadcast(f32[32,4,8]{2,1,0:T(4,128)S(1)} %copy.43), dimensions={0,1,3} | broadcast | bytes 2101248 | tf_op jit(solution)/shard_map/broadcast_in_dim | solution.py:164
  242.4 7.1 %reshape.102 = f32[32,64,256]{2,1,0:T(8,128)} reshape(f32[32,4,16,8,32]{4,3,2,1,0:T(8,128)} %broadcast_in_dim.18) | data formatting | bytes 4194304 | tf_op jit(solution)/shard_map/reshape | solution.py:172
  252.2 2.3 copy.40
  259.1 13.5 %fusion.4 = f32[32,64,256]{2,1,0:T(8,128)S(1)} fusion(f32[32,64,256]{2,1,0:T(8,128)} %reshape.102, f32[35,66,1]{2,1,0:T(8,128)} %copy.39, f32[35,1,256]{2,1,0:T(1,128)} %copy-done.13, f32[35,64,256]{2,1,0:T(8,128)} %copy-done, f32[35,1,256]{2,1,0:T(1,128)} %copy-done.14, f32[32,66,258]{2,1,0:T(8,128)S(1)} %add_divide_fusion.1, f32[35,66,1]{2,1,0:T(8,128)} %copy.40, ...), kind=kLoop, calls=%fused_computation.11 | loop fusion | flops 25165824 | bytes 19554992 | tf_op jit(solution)/shard_map/add | solution.py:168
  274.1 1.8 fusion.85
  275.9 3.0 collective-permute-done.5
  279.1 1.9 collective-permute-start.7
  281.1 3.9 %collective-permute-start.6 = (f32[35,1,256]{2,1,0:T(1,128)S(1)}, f32[35,1,256]{2,1,0:T(1,128)S(1)}, u32[]{:S(2)}, u32[]{:S(2)}) collective-permute-start(f32[35,1,256]{2,1,0:T(1,128)S(1)} %get-tuple-element.12), channel_id=1, source_target_pairs={{0,16},{16,32},{32,48},{1,17},{17,33},{33,49},{2,18},{18,34},{34,5... | collective-permute-start | bytes 107528 | tf_op jit(solution)/shard_map/ppermute | solution.py:30
  285.1 3.9 %broadcast_in_dim.20 = f32[32,4,16,8,32]{4,3,2,1,0:T(8,128)} broadcast(f32[32,4,8]{2,1,0:T(4,128)S(1)} %copy.50), dimensions={0,1,3} | broadcast | bytes 2101248 | tf_op jit(solution)/shard_map/broadcast_in_dim | solution.py:164
  289.0 7.0 %reshape.104 = f32[32,64,256]{2,1,0:T(8,128)} reshape(f32[32,4,16,8,32]{4,3,2,1,0:T(8,128)} %broadcast_in_dim.20) | data formatting | bytes 4194304 | tf_op jit(solution)/shard_map/reshape | solution.py:172
  296.4 1.9 fusion.81
  298.2 1.8 copy.44
  301.3 1.8 copy.45
  304.4 12.7 %all_gather.17 = f32[4,64,256]{2,1,0:T(8,128)S(1)} all-gather(f32[1,64,256]{2,1,0:T(8,128)S(1)} %get-tuple-element.16), channel_id=1, replica_groups=mesh['coh'=4,'lat'=4,'lon'=16] {'coh'}, dimensions={0}, use_global_device_ids=true | all-gather | bytes 327680 | tf_op jit(solution)/shard_map/all_gather | solution.py:14
  325.0 9.0 %fusion.6 = f32[32,64,256]{2,1,0:T(8,128)} fusion(f32[32,64,256]{2,1,0:T(8,128)S(1)} %copy-done.6, f32[35,66,1]{2,1,0:T(8,128)S(1)} %copy-done.1, f32[35,1,256]{2,1,0:T(1,128)S(1)} %collective-permute-done.7, f32[35,64,256]{2,1,0:T(8,128)S(1)} %bitcast_dynamic-update-slice_fusion, f32[35,1,256]{2,1,0:T(1,128)S(1)} %collective-permute-done.6, ...), kind=kLoop, calls=%fused_computation.13 | loop fusion | flops 25165824 | bytes 19554992 | tf_op jit(solution)/shard_map/add | solution.py:168
  (134 shorter events, 38.5 us)
Async XLA Ops:
  7.2 250.7 %all-reduce.3.cloned.1.call-start = ((), (), s32[]{:S(2)}) async-start(), calls=%async_computation | async-start | bytes 262144 | tf_op jit(solution)/shard_map/psum | solution.py:118
  8.7 3.7 %copy-start.7 = (f32[32,64,256]{2,1,0:T(8,128)}, f32[32,64,256]{2,1,0:T(8,128)S(1)}, u32[]{:S(2)}) copy-start(f32[32,64,256]{2,1,0:T(8,128)S(1)} %convert_element_type.33) | copy-start | bytes 6291460
  9.4 173.3 %collective-permute-start = (f32[64,256]{1,0:T(8,128)}, f32[64,256]{1,0:T(8,128)S(1)}, u32[]{:S(2)}, u32[]{:S(2)}) collective-permute-start(f32[64,256]{1,0:T(8,128)} %get-tuple-element.23), channel_id=1, source_target_pairs={{64,0},{128,64},{192,128},{65,1},{129,65},{193,129},{66,2},{130,66... | collective-permute-start | bytes 196616 | tf_op jit(solution)/shard_map/ppermute | solution.py:20
  12.4 2.7 copy-start.22
  16.9 167.6 %copy-start.10 = (s32[64,256]{1,0:T(8,128)S(1)}, s32[64,256]{1,0:T(8,128)}, u32[]{:S(2)}) copy-start(s32[64,256]{1,0:T(8,128)} %param.22) | copy-start | bytes 196612
  182.8 24.1 %copy-start.17 = (f32[64,256]{1,0:T(8,128)}, f32[64,256]{1,0:T(8,128)S(1)}, u32[]{:S(2)}) copy-start(f32[64,256]{1,0:T(8,128)S(1)} %collective-permute-done) | copy-start | bytes 196612
  184.5 71.1 %copy-start = (f32[35,64,256]{2,1,0:T(8,128)}, f32[35,64,256]{2,1,0:T(8,128)S(1)}, u32[]{:S(2)}) copy-start(f32[35,64,256]{2,1,0:T(8,128)S(1)} %bitcast_dynamic-update-slice_fusion.1) | copy-start | bytes 6881284
  184.6 24.3 %collective-permute-start.2 = (f32[35,1,256]{2,1,0:T(1,128)S(1)}, f32[35,1,256]{2,1,0:T(1,128)S(1)}, u32[]{:S(2)}, u32[]{:S(2)}) collective-permute-start(f32[35,1,256]{2,1,0:T(1,128)S(1)} %get-tuple-element.15), channel_id=1, source_target_pairs={{16,0},{32,16},{48,32},{17,1},{33,17},{49,33},{18,2},{34,18},{50,3... | collective-permute-start | bytes 107528 | tf_op jit(solution)/shard_map/ppermute | solution.py:31
  206.9 5.8 %collective-permute-start.1 = (f32[35,1,256]{2,1,0:T(1,128)S(1)}, f32[35,1,256]{2,1,0:T(1,128)S(1)}, u32[]{:S(2)}, u32[]{:S(2)}) collective-permute-start(f32[35,1,256]{2,1,0:T(1,128)S(1)} %get-tuple-element.14), channel_id=1, source_target_pairs={{0,16},{16,32},{32,48},{1,17},{17,33},{33,49},{2,18},{18,34},{34,5... | collective-permute-start | bytes 107528 | tf_op jit(solution)/shard_map/ppermute | solution.py:30
  208.9 46.7 %copy-start.13 = (f32[35,1,256]{2,1,0:T(1,128)}, f32[35,1,256]{2,1,0:T(1,128)S(1)}, u32[]{:S(2)}) copy-start(f32[35,1,256]{2,1,0:T(1,128)S(1)} %collective-permute-done.2) | copy-start | bytes 107524
  212.7 42.9 %copy-start.14 = (f32[35,1,256]{2,1,0:T(1,128)}, f32[35,1,256]{2,1,0:T(1,128)S(1)}, u32[]{:S(2)}) copy-start(f32[35,1,256]{2,1,0:T(1,128)S(1)} %collective-permute-done.1) | copy-start | bytes 107524
  215.0 21.8 %copy-start.5 = (bf16[32,64,256]{2,1,0:T(8,128)(2,1)S(1)}, bf16[32,64,256]{2,1,0:T(8,128)(2,1)}, u32[]{:S(2)}) copy-start(bf16[32,64,256]{2,1,0:T(8,128)(2,1)} %param.19) | copy-start | bytes 3145732
  216.8 33.8 %collective-permute-start.3 = (f32[35,66,1]{1,2,0:T(1,128)S(1)}, f32[35,66,1]{1,2,0:T(1,128)S(1)}, u32[]{:S(2)}, u32[]{:S(2)}) collective-permute-start(f32[35,66,1]{1,2,0:T(1,128)S(1)} %copy.37), channel_id=1, source_target_pairs={{0,1},{1,2},{2,3},{3,4},{4,5},{5,6},{6,7},{7,8},{8,9},{9,10},{10,1... | collective-permute-start | bytes 27728 | tf_op jit(solution)/shard_map/ppermute | solution.py:30
  220.5 31.7 %collective-permute-start.4 = (f32[35,66,1]{1,2,0:T(1,128)}, f32[35,66,1]{1,2,0:T(1,128)}, u32[]{:S(2)}, u32[]{:S(2)}) collective-permute-start(f32[35,66,1]{1,2,0:T(1,128)} %copy.38), channel_id=1, source_target_pairs={{1,0},{2,1},{3,2},{4,3},{5,4},{6,5},{7,6},{8,7},{9,8},{10,9},{11,1... | collective-permute-start | bytes 27728 | tf_op jit(solution)/shard_map/ppermute | solution.py:31
  242.4 7.1 %copy-start.9 = (f32[4,64,256]{2,1,0:T(8,128)S(1)}, f32[4,64,256]{2,1,0:T(8,128)}, u32[]{:S(2)}) copy-start(f32[4,64,256]{2,1,0:T(8,128)} %all_gather.14) | copy-start | bytes 786436
  242.4 7.7 %copy-start.32 = (f32[32]{0:T(128)S(1)}, f32[32]{0:T(128)}, u32[]{:S(2)}) copy-start(f32[32]{0:T(128)} %param.25) | copy-start | bytes 388
  272.7 6.3 %copy-start.19 = (f32[2,64,256]{2,1,0:T(8,128)S(1)}, f32[2,64,256]{2,1,0:T(8,128)}, u32[]{:S(2)}) copy-start(f32[2,64,256]{2,1,0:T(8,128)} %param.20) | copy-start | bytes 393220
  272.7 6.3 %copy-start.20 = (f32[2,64,256]{2,1,0:T(8,128)S(1)}, f32[2,64,256]{2,1,0:T(8,128)}, u32[]{:S(2)}) copy-start(f32[2,64,256]{2,1,0:T(8,128)} %param.21) | copy-start | bytes 393220
  272.7 6.4 %copy-start.11 = (s32[64,256]{1,0:T(8,128)S(1)}, s32[64,256]{1,0:T(8,128)}, u32[]{:S(2)}) copy-start(s32[64,256]{1,0:T(8,128)} %param.22) | copy-start | bytes 196612
  272.7 6.3 %collective-permute-start.5 = (f32[64,256]{1,0:T(8,128)S(1)}, f32[64,256]{1,0:T(8,128)S(1)}, u32[]{:S(2)}, u32[]{:S(2)}) collective-permute-start(f32[64,256]{1,0:T(8,128)S(1)} %get-tuple-element.17), channel_id=1, source_target_pairs={{64,0},{128,64},{192,128},{65,1},{129,65},{193,129},{66,2},{130,66... | collective-permute-start | bytes 196616 | tf_op jit(solution)/shard_map/ppermute | solution.py:20
  279.1 16.9 %collective-permute-start.7 = (f32[35,1,256]{2,1,0:T(1,128)S(1)}, f32[35,1,256]{2,1,0:T(1,128)S(1)}, u32[]{:S(2)}, u32[]{:S(2)}) collective-permute-start(f32[35,1,256]{2,1,0:T(1,128)S(1)} %get-tuple-element.13), channel_id=1, source_target_pairs={{16,0},{32,16},{48,32},{17,1},{33,17},{49,33},{18,2},{34,18},{50,3... | collective-permute-start | bytes 107528 | tf_op jit(solution)/shard_map/ppermute | solution.py:31
  281.1 15.0 %collective-permute-start.6 = (f32[35,1,256]{2,1,0:T(1,128)S(1)}, f32[35,1,256]{2,1,0:T(1,128)S(1)}, u32[]{:S(2)}, u32[]{:S(2)}) collective-permute-start(f32[35,1,256]{2,1,0:T(1,128)S(1)} %get-tuple-element.12), channel_id=1, source_target_pairs={{0,16},{16,32},{32,48},{1,17},{17,33},{33,49},{2,18},{18,34},{34,5... | collective-permute-start | bytes 107528 | tf_op jit(solution)/shard_map/ppermute | solution.py:30
  300.0 17.1 %collective-permute-start.8 = (f32[35,66,1]{1,2,0:T(1,128)S(1)}, f32[35,66,1]{1,2,0:T(1,128)S(1)}, u32[]{:S(2)}, u32[]{:S(2)}) collective-permute-start(f32[35,66,1]{1,2,0:T(1,128)S(1)} %copy.44), channel_id=1, source_target_pairs={{0,1},{1,2},{2,3},{3,4},{4,5},{5,6},{6,7},{7,8},{8,9},{9,10},{10,1... | collective-permute-start | bytes 27728 | tf_op jit(solution)/shard_map/ppermute | solution.py:30
  303.1 15.6 %collective-permute-start.9 = (f32[35,66,1]{1,2,0:T(1,128)S(1)}, f32[35,66,1]{1,2,0:T(1,128)S(1)}, u32[]{:S(2)}, u32[]{:S(2)}) collective-permute-start(f32[35,66,1]{1,2,0:T(1,128)S(1)} %copy.45), channel_id=1, source_target_pairs={{1,0},{2,1},{3,2},{4,3},{5,4},{6,5},{7,6},{8,7},{9,8},{10,9},{11,1... | collective-permute-start | bytes 27728 | tf_op jit(solution)/shard_map/ppermute | solution.py:31
  (20 other events, 34.3 us)
Sparse Core Ops, SparseCore 0:
  15.2 50.6 all-reduce.2
